TPU v7x, 512 devices: a whole 4x8x8 slice. The times are simulated.
512 devices in a mesh: seq: 64 (over z, x, core), head: 8 (over y).
Axes of the slice: x: 4, y: 8, z: 8, core: 2. Of those that a mesh axis runs over, the one named last changes fastest.
Arguments:
- query_states: bfloat16 [16384, 4096], P(('seq', 'head')), may hold values from -8 to 8
- key_states: bfloat16 [16384, 4096], P(('seq', 'head')), may hold values from -8 to 8
- value_states: bfloat16 [16384, 4096], P(('seq', 'head')), may hold values from -8 to 8
- out_grad: bfloat16 [16384, 4096], P(('seq', 'head')), may hold values from -6 to 6
Outputs:
- attended: bfloat16 [16384, 4096], P('seq', 'head')
- query_grad: bfloat16 [16384, 4096], P('seq', 'head')
- key_grad: bfloat16 [16384, 4096], P('seq', 'head')
- value_grad: bfloat16 [16384, 4096], P('seq', 'head')
All inputs are finite; a program needn't handle non-finite values.
Results may differ from a plain program's by a relative error of at most 0.025.
Values may be sent and summed in bfloat16 or wider, within the bound.
A program may use at most 64 MiB of HBM per device.

v0:
```python
import jax
import jax.numpy as jnp
import numpy as np
from jax import lax
from jax.sharding import Mesh
from jax.sharding import PartitionSpec as P

HEAD_DIM = 128
BLOCK = 128


def seq_parts(mesh):
    column = mesh.devices[:, 0]
    count = column.shape[0]
    try:
        cores = len({d.core_on_chip for d in column})
        xs = len({d.coords[0] for d in column})
    except AttributeError:
        return (("s0", count),)
    parts = [("sz", count // (xs * cores)), ("sx", xs), ("sc", cores)]
    if parts[0][1] * xs * cores != count:
        return (("s0", count),)
    return tuple((p for p in parts if p[1] > 1)) or (("s0", count),)


def make_local(parts):
    seq = tuple((name for name, _ in parts))
    seq_count = int(np.prod([size for _, size in parts]))

    def hpsum(value):
        for name in reversed(seq):
            value = lax.psum(value, name)
        return value

    def hgather(value):
        for name in reversed(seq):
            value = lax.all_gather(value, name, axis=0, tiled=True)
        return value

    def shifted(value, steps):
        leading, last = (max(0, -steps), min(seq_count, seq_count - steps))
        return lax.ppermute(value, seq, [(s, s + steps) for s in range(leading, last)])

    def local(query_states, key_states, value_states, out_grad):
        stacked = jnp.stack([query_states, key_states, value_states, out_grad])
        stacked = lax.all_to_all(stacked, "head", split_axis=2, concat_axis=1, tiled=True)
        local_rows = stacked.shape[1]
        head_count = stacked.shape[2] // HEAD_DIM
        block_count = local_rows // BLOCK
        position = lax.axis_index(seq)
        total_blocks = block_count * seq_count
        inverse_square_root = HEAD_DIM ** (-0.5)
        query_states, key_states, value_states, out_grad = (
            stacked[0],
            stacked[1],
            stacked[2],
            stacked[3],
        )

        def as_blocks(array):
            return array.reshape(block_count, BLOCK, head_count, HEAD_DIM)

        def as_heads(array):
            return array.reshape(array.shape[0], head_count, HEAD_DIM)

        leading = stacked[:, :BLOCK]
        leading = jnp.where(position == 0, leading, jnp.zeros_like(leading))
        leading = hpsum(leading)
        glob_query = as_heads(leading[0])
        glob_key = as_heads(leading[1])
        glob_value = as_heads(leading[2])
        glob_grad = as_heads(leading[3])
        kv = stacked[1:3]
        from_before = shifted(kv[:, local_rows - BLOCK :], 1)
        from_after = shifted(kv[:, :BLOCK], -1)
        extended = jnp.concatenate([from_before, kv, from_after], axis=1)

        def windows(rows_ext, shared):
            spread = jnp.broadcast_to(shared[None], (block_count, BLOCK, head_count, HEAD_DIM))
            return jnp.concatenate(
                [
                    spread,
                    as_blocks(rows_ext[:local_rows]),
                    as_blocks(rows_ext[BLOCK : BLOCK + local_rows]),
                    as_blocks(rows_ext[2 * BLOCK :]),
                ],
                1,
            )

        window_key_rows = windows(extended[0], glob_key)
        window_value_rows = windows(extended[1], glob_value)
        block_ids = position * block_count + jnp.arange(block_count)
        allowed = jnp.stack(
            [block_ids >= 2, block_ids >= 1, block_ids >= 0, block_ids + 1 < total_blocks], 1
        )
        allowed = jnp.repeat(allowed, BLOCK, axis=1)[:, None, None, :]
        live_rows = (block_ids != 0)[:, None, None, None]
        query_blocks = as_blocks(query_states)
        grad_blocks = as_blocks(out_grad)
        logit_scores = (
            jnp.einsum(
                "cqhd,ckhd->chqk", query_blocks, window_key_rows, preferred_element_type=jnp.float32
            )
            * inverse_square_root
        )
        logit_scores = jnp.where(allowed, logit_scores, -1e30)
        row_top = jnp.max(logit_scores, -1, keepdims=True)
        log_total = row_top + jnp.log(jnp.sum(jnp.exp(logit_scores - row_top), -1, keepdims=True))
        weights = jnp.where(allowed & live_rows, jnp.exp(logit_scores - log_total), 0.0)
        probabilities = weights.astype(jnp.bfloat16)
        window_output = jnp.einsum(
            "chqk,ckhd->cqhd", probabilities, window_value_rows, preferred_element_type=jnp.float32
        ).astype(jnp.bfloat16)
        local_keys = as_heads(key_states)
        local_values = as_heads(value_states)
        glob_scores = (
            jnp.einsum("qhd,khd->hqk", glob_query, local_keys, preferred_element_type=jnp.float32)
            * inverse_square_root
        )
        local_top = jnp.max(glob_scores, -1)
        local_exp = jnp.exp(glob_scores - local_top[:, :, None])
        local_sum = jnp.sum(local_exp, -1)
        local_out = jnp.einsum(
            "hqk,khd->hqd",
            local_exp,
            local_values.astype(jnp.float32),
            preferred_element_type=jnp.float32,
        )
        local_delta = jnp.sum(local_out * glob_grad.astype(jnp.float32).transpose(1, 0, 2), -1)
        stats = hgather(jnp.stack([local_top, local_sum, local_delta])[None])
        glob_top = jnp.max(stats[:, 0], 0)
        rescale = jnp.exp(stats[:, 0] - glob_top[None])
        glob_total = jnp.sum(rescale * stats[:, 1], 0)
        glob_log = glob_top + jnp.log(glob_total)
        glob_delta = jnp.sum(rescale * stats[:, 2], 0) / glob_total
        glob_weights = jnp.exp(glob_scores - glob_log[:, :, None])
        glob_probs = glob_weights.astype(jnp.bfloat16)
        glob_part = jnp.einsum(
            "hqk,khd->qhd", glob_probs, local_values, preferred_element_type=jnp.float32
        )
        glob_dprob = jnp.einsum(
            "qhd,khd->hqk", glob_grad, local_values, preferred_element_type=jnp.float32
        )
        glob_dscore = (glob_weights * (glob_dprob - glob_delta[:, :, None])).astype(jnp.bfloat16)
        glob_dquery_part = (
            jnp.einsum("hqk,khd->qhd", glob_dscore, local_keys, preferred_element_type=jnp.float32)
            * inverse_square_root
        )
        key_from_glob = (
            jnp.einsum("hqk,qhd->khd", glob_dscore, glob_query, preferred_element_type=jnp.float32)
            * inverse_square_root
        )
        value_from_glob = jnp.einsum(
            "hqk,qhd->khd", glob_probs, glob_grad, preferred_element_type=jnp.float32
        )
        band_delta = jnp.sum(
            grad_blocks.astype(jnp.float32) * window_output.astype(jnp.float32), -1
        ).transpose(0, 2, 1)
        probability_gradient = jnp.einsum(
            "cqhd,ckhd->chqk", grad_blocks, window_value_rows, preferred_element_type=jnp.float32
        )
        score_gradient = (weights * (probability_gradient - band_delta[:, :, :, None])).astype(
            jnp.bfloat16
        )
        window_query_gradient = (
            jnp.einsum(
                "chqk,ckhd->cqhd",
                score_gradient,
                window_key_rows,
                preferred_element_type=jnp.float32,
            )
            * inverse_square_root
        )
        window_key_gradient = (
            jnp.einsum(
                "chqk,cqhd->ckhd", score_gradient, query_blocks, preferred_element_type=jnp.float32
            )
            * inverse_square_root
        )
        window_value_gradient = jnp.einsum(
            "chqk,cqhd->ckhd", probabilities, grad_blocks, preferred_element_type=jnp.float32
        )
        stacked_grads = jnp.stack([window_key_gradient, window_value_gradient]).reshape(
            2, block_count, 4, BLOCK, head_count, HEAD_DIM
        )
        glob_piece = jnp.sum(stacked_grads[:, :, 0], 1)
        before = stacked_grads[:, :, 1]
        middle = stacked_grads[:, :, 2]
        after = stacked_grads[:, :, 3]
        empty_block = jnp.zeros((2, 1, BLOCK, head_count, HEAD_DIM), jnp.float32)
        inner = (
            middle
            + jnp.concatenate([before[:, 1:], empty_block], 1)
            + jnp.concatenate([empty_block, after[:, :-1]], 1)
        )
        from_right = shifted(before[:, 0].astype(jnp.bfloat16), -1).astype(jnp.float32)
        from_left = shifted(after[:, -1].astype(jnp.bfloat16), 1).astype(jnp.float32)
        inner = inner.at[:, 0].add(from_left)
        inner = inner.at[:, -1].add(from_right)
        glob_out, glob_dquery, glob_dkey, glob_dvalue = hpsum(
            (glob_part, glob_dquery_part, glob_piece[0], glob_piece[1])
        )
        glob_out = glob_out.astype(jnp.bfloat16)
        local_grads = inner.reshape(2, local_rows, head_count, HEAD_DIM) + jnp.stack(
            [key_from_glob, value_from_glob]
        )
        is_first = ((jnp.arange(local_rows) < BLOCK) & (position == 0))[:, None, None]

        def padded(array):
            return jnp.concatenate(
                [array, jnp.zeros((local_rows - BLOCK,) + array.shape[1:], array.dtype)], 0
            )

        key_grad = local_grads[0] + jnp.where(is_first, padded(glob_dkey), 0.0)
        value_grad = local_grads[1] + jnp.where(is_first, padded(glob_dvalue), 0.0)
        query_grad = jnp.where(
            is_first,
            padded(glob_dquery),
            window_query_gradient.reshape(local_rows, head_count, HEAD_DIM),
        )
        attended = jnp.where(
            is_first, padded(glob_out), window_output.reshape(local_rows, head_count, HEAD_DIM)
        )
        return (
            attended.reshape(local_rows, -1),
            query_grad.reshape(local_rows, -1).astype(jnp.bfloat16),
            key_grad.reshape(local_rows, -1).astype(jnp.bfloat16),
            value_grad.reshape(local_rows, -1).astype(jnp.bfloat16),
        )

    return (local, seq)


def solution(mesh):
    parts = seq_parts(mesh)
    heads = mesh.shape["head"]
    names = tuple((name for name, _ in parts))
    sizes = tuple((size for _, size in parts))
    split_mesh = Mesh(mesh.devices.reshape(sizes + (heads,)), names + ("head",))
    local, seq = make_local(parts)
    spec_in = P(seq + ("head",), None)
    spec_out = P(seq, "head")
    return jax.shard_map(
        local, mesh=split_mesh, in_specs=(spec_in,) * 4, out_specs=(spec_out,) * 4, check_vma=False
    )
```

profile of v0, /device:TPU:2, one launch (start us, length us, event | category | flops | bytes accessed | tf_op | source)
XLA Modules:
  0.0 490.2 jit_solution(11910787131558376043)
XLA Ops:
  8.5 4.6 copy.152
  13.1 7.8 %reshape.257 = bf16[8,2,32768]{2,1,0:T(2,128)(2,1)} reshape(bf16[4096,4,32]{2,1,0:T(4,128)(2,1)} %bitcast.155) | data formatting | bytes 2097152
  20.9 7.1 %all-to-all-start = ((bf16[8,2,32768]{2,1,0:T(2,128)(2,1)}), bf16[8,2,32768]{2,1,0:T(2,128)(2,1)S(1)}, u32[]{:S(2)}, u32[]{:S(2)}) async-start(bf16[8,2,32768]{2,1,0:T(2,128)(2,1)} %reshape.257), calls=%async_computation | async-start | bytes 2097152 | tf_op jit(solution)/shard_map/all_to_all | solution.py:46
  28.1 28.7 %all-to-all-done = bf16[8,2,32768]{2,1,0:T(2,128)(2,1)S(1)} async-done(((bf16[8,2,32768]{2,1,0:T(2,128)(2,1)}), bf16[8,2,32768]{2,1,0:T(2,128)(2,1)S(1)}, u32[]{:S(2)}, u32[]{:S(2)}) %all-to-all-start) | async-done | bytes 1048608 | tf_op jit(solution)/shard_map/all_to_all | solution.py:46
  56.8 4.5 reshape.258
  61.3 5.5 %copy.199 = bf16[4,32,8,512]{3,1,2,0:T(8,128)(2,1)S(1)} copy(bf16[4,32,8,512]{1,0,3,2:T(4,128)(2,1)} %bitcast.153) | data formatting | bytes 2097152 | tf_op jit(solution)/shard_map/all_to_all | solution.py:46
  67.7 34.6 %all-reduce.18.cloned.1.call-done = bf16[4,128,512]{2,1,0:T(8,128)(2,1)} async-done(((bf16[4,128,512]{2,1,0:T(8,128)(2,1)}), bf16[4,128,512]{2,1,0:T(8,128)(2,1)}) %all-reduce.18.cloned.1.call-update) | async-done | bytes 524304 | tf_op jit(solution)/shard_map/psum | solution.py:32
  102.5 4.7 copy.198
  107.5 2.2 collective-permute-start
  109.7 3.4 collective-permute-start.1
  113.1 46.0 %all-reduce.20.cloned.1.call-done = bf16[4,128,512]{2,1,0:T(8,128)(2,1)} async-done(((bf16[4,128,512]{2,1,0:T(8,128)(2,1)}), bf16[4,128,512]{2,1,0:T(8,128)(2,1)}) %all-reduce.20.cloned.1.call-update) | async-done | bytes 524304 | tf_op jit(solution)/shard_map/psum | solution.py:32
  164.3 78.4 %all-reduce.22.cloned.1.call-done = bf16[4,128,512]{2,1,0:T(8,128)(2,1)} async-done(((bf16[4,128,512]{2,1,0:T(8,128)(2,1)}), bf16[4,128,512]{2,1,0:T(8,128)(2,1)}) %all-reduce.22.cloned.1.call-update) | async-done | bytes 524304 | tf_op jit(solution)/shard_map/psum | solution.py:32
  245.8 1.8 all-gather
  247.7 11.9 %all_gather.10 = f32[8,3,4,128]{3,2,1,0:T(4,128)S(1)} all-gather(f32[2,3,4,128]{3,2,1,0:T(4,128)S(1)} %bitcast.176), channel_id=1, replica_groups=mesh['sz'=8,'sx'=4,'sc'=2,'head'=8] {'sx'}, dimensions={0}, use_global_device_ids=true | all-gather | bytes 61440 | tf_op jit(solution)/shard_map/all_gather | solution.py:37
  259.6 25.1 %all_gather.11 = f32[64,3,4,128]{3,2,1,0:T(4,128)S(1)} all-gather(f32[8,3,4,128]{3,2,1,0:T(4,128)S(1)} %all_gather.10), channel_id=1, replica_groups=mesh['sz'=8,'sx'=4,'sc'=2,'head'=8] {'sz'}, dimensions={0}, use_global_device_ids=true | all-gather | bytes 442368 | tf_op jit(solution)/shard_map/all_gather | solution.py:37
  297.7 2.0 copy_dynamic-update-slice_fusion.1
  304.7 1.9 collective-permute-start.2
  307.4 3.6 collective-permute-start.3
  311.1 25.9 %all-reduce.28.cloned.1.call-done = (f32[128,4,128]{0,2,1:T(8,128)}, f32[128,4,128]{0,2,1:T(8,128)}, f32[128,4,128]{0,2,1:T(8,128)}, f32[128,4,128]{0,2,1:T(8,128)}) async-done(((f32[128,4,128]{0,2,1:T(8,128)}, f32[128,4,128]{0,2,1:T(8,128)}, f32[128,4,128]{0,2,1:T(8,128)}, f32[128,4,128]{0,2,1:T(8,128)}), (f32[128,4,128]{0,2,1:T(8,128)}, f32[128,4,128]{0,2,1:T(8,128)}, f32[128,4,128]{0,2,1:T(8,128)}, ...) | async-done | bytes 1048592 | tf_op jit(solution)/shard_map/psum | solution.py:32
  337.2 2.6 fusion.1
  347.2 12.0 %scatter-add.9 = f32[2,2,128,4,128]{2,1,4,3,0:T(2,128)S(1)} dynamic-update-slice(f32[2,2,128,4,128]{2,1,4,3,0:T(2,128)S(1)} %copy.191, f32[2,1,128,4,128]{2,1,4,3,0:T(1,128)S(1)} %add.147, s32[]{:T(128)} %constant.93.clone.1, s32[]{:T(128)} %constant.98.clone.1, s32[]{:T(128)} %constant.93.clone.1, s32[]{:T(128)} %constant.93.clone.1, s32[]{:T(128)} %constant.93.clone.1) | dynamic-update-slice | bytes 1048580 | tf_op jit(solution)/shard_map/scatter-add | solution.py:199
  360.1 37.1 %all-reduce.26.cloned.1.call-done = (f32[128,4,128]{0,2,1:T(8,128)}, f32[128,4,128]{0,2,1:T(8,128)}, f32[128,4,128]{0,2,1:T(8,128)}, f32[128,4,128]{0,2,1:T(8,128)}) async-done(((f32[128,4,128]{0,2,1:T(8,128)}, f32[128,4,128]{0,2,1:T(8,128)}, f32[128,4,128]{0,2,1:T(8,128)}, f32[128,4,128]{0,2,1:T(8,128)}), (f32[128,4,128]{0,2,1:T(8,128)}, f32[128,4,128]{0,2,1:T(8,128)}, f32[128,4,128]{0,2,1:T(8,128)}, ...) | async-done | bytes 1048592 | tf_op jit(solution)/shard_map/psum | solution.py:32
  398.5 39.7 %all-reduce.29 = (bf16[128,4,128]{0,2,1:T(8,128)(2,1)S(1)}, bf16[128,4,128]{0,2,1:T(8,128)(2,1)S(1)}) all-reduce(f32[128,4,128]{0,2,1:T(8,128)S(1)} %copy-done.14, f32[128,4,128]{0,2,1:T(8,128)} %get-tuple-element.55), channel_id=1, replica_groups=mesh['sz'=8,'sx'=4,'sc'=2,'head'=8] {'sz'}, use_global_device_ids=true, to_apply=%region_10.11 | all-reduce | flops 131072 | bytes 786432 | tf_op jit(solution)/shard_map/psum | solution.py:32
  440.0 40.6 %all-reduce.24.cloned.1.call-done = (f32[128,4,128]{0,2,1:T(8,128)}, f32[128,4,128]{0,2,1:T(8,128)}) async-done(((f32[128,4,128]{0,2,1:T(8,128)}, f32[128,4,128]{0,2,1:T(8,128)}), (f32[128,4,128]{0,2,1:T(8,128)}, f32[128,4,128]{0,2,1:T(8,128)})) %all-reduce.24.cloned.1.call-update) | async-done | bytes 524304 | tf_op jit(solution)/shard_map/psum | solution.py:32
  (144 shorter events, 43.8 us)
Async XLA Ops:
  20.9 35.8 %all-to-all-start = ((bf16[8,2,32768]{2,1,0:T(2,128)(2,1)}), bf16[8,2,32768]{2,1,0:T(2,128)(2,1)S(1)}, u32[]{:S(2)}, u32[]{:S(2)}) async-start(bf16[8,2,32768]{2,1,0:T(2,128)(2,1)} %reshape.257), calls=%async_computation | async-start | bytes 2097152 | tf_op jit(solution)/shard_map/all_to_all | solution.py:46
  28.0 74.3 %all-reduce.18.cloned.1.call-start = ((), (), s32[]{:S(2)}) async-start(), calls=%async_computation.1 | async-start | bytes 1048576 | tf_op jit(solution)/shard_map/psum | solution.py:32
  67.6 91.4 %all-reduce.20.cloned.1.call-start = ((), (), s32[]{:S(2)}) async-start(), calls=%async_computation.2 | async-start | bytes 1048576 | tf_op jit(solution)/shard_map/psum | solution.py:32
  102.3 140.3 %all-reduce.22.cloned.1.call-start = ((), (), s32[]{:S(2)}) async-start(), calls=%async_computation.3 | async-start | bytes 1048576 | tf_op jit(solution)/shard_map/psum | solution.py:32
  107.5 53.7 %collective-permute-start = (bf16[2,128,512]{2,1,0:T(8,128)(2,1)S(1)}, bf16[2,128,512]{2,1,0:T(8,128)(2,1)}, u32[]{:S(2)}, u32[]{:S(2)}) collective-permute-start(bf16[2,128,512]{2,1,0:T(8,128)(2,1)S(1)} %get-tuple-element.83), channel_id=1, source_target_pairs={{0,8},{8,16},{16,24},{24,32},{32,40},{40,48},{48,56},{56,64},{64,7... | collective-permute-start | bytes 786440 | tf_op jit(solution)/shard_map/ppermute | solution.py:42
  109.7 51.5 %collective-permute-start.1 = (bf16[2,128,512]{2,1,0:T(8,128)(2,1)S(1)}, bf16[2,128,512]{2,1,0:T(8,128)(2,1)}, u32[]{:S(2)}, u32[]{:S(2)}) collective-permute-start(bf16[2,128,512]{2,1,0:T(8,128)(2,1)S(1)} %get-tuple-element.84), channel_id=1, source_target_pairs={{8,0},{16,8},{24,16},{32,24},{40,32},{48,40},{56,48},{64,56},{72,6... | collective-permute-start | bytes 786440 | tf_op jit(solution)/shard_map/ppermute | solution.py:42
  159.1 177.9 %all-reduce.28.cloned.1.call-start = ((), (), s32[]{:S(2)}) async-start(), calls=%async_computation.6 | async-start | bytes 2097152 | tf_op jit(solution)/shard_map/psum | solution.py:32
  160.7 126.5 %copy-start.9 = (bf16[2,128,4,128]{3,1,2,0:T(8,128)(2,1)}, bf16[2,128,4,128]{3,1,2,0:T(8,128)(2,1)S(1)}, u32[]{:S(2)}) copy-start(bf16[2,128,4,128]{3,1,2,0:T(8,128)(2,1)S(1)} %copy.175) | copy-start | bytes 786436
  162.5 124.7 %copy-start.10 = (bf16[2,128,4,128]{3,1,2,0:T(8,128)(2,1)}, bf16[2,128,4,128]{3,1,2,0:T(8,128)(2,1)S(1)}, u32[]{:S(2)}) copy-start(bf16[2,128,4,128]{3,1,2,0:T(8,128)(2,1)S(1)} %copy.174) | copy-start | bytes 786436
  164.3 122.9 %copy-start.11 = (bf16[2,128,4,128]{3,1,2,0:T(8,128)(2,1)}, bf16[2,128,4,128]{3,1,2,0:T(8,128)(2,1)S(1)}, u32[]{:S(2)}) copy-start(bf16[2,128,4,128]{3,1,2,0:T(8,128)(2,1)S(1)} %copy.176) | copy-start | bytes 786436
  244.8 41.1 %copy-start.3 = (bf16[1,128,512]{1,2,0:T(8,128)(2,1)}, bf16[1,128,512]{1,2,0:T(8,128)(2,1)S(1)}, u32[]{:S(2)}) copy-start(bf16[1,128,512]{1,2,0:T(8,128)(2,1)S(1)} %copy.156) | copy-start | bytes 393220
  297.7 2.2 copy-start.1
  300.2 2.0 copy-start
  303.0 94.3 %all-reduce.26.cloned.1.call-start = ((), (), s32[]{:S(2)}) async-start(), calls=%async_computation.5 | async-start | bytes 2097152 | tf_op jit(solution)/shard_map/psum | solution.py:32
  304.7 40.0 %collective-permute-start.2 = (bf16[2,128,4,128]{1,3,2,0:T(8,128)(2,1)}, bf16[2,128,4,128]{1,3,2,0:T(8,128)(2,1)S(1)}, u32[]{:S(2)}, u32[]{:S(2)}) collective-permute-start(bf16[2,128,4,128]{1,3,2,0:T(8,128)(2,1)} %fusion.17), channel_id=1, source_target_pairs={{0,8},{8,16},{16,24},{24,32},{32,40},{40,48},{48,56},{56,64},{64,7... | collective-permute-start | bytes 786440 | tf_op jit(solution)/shard_map/ppermute | solution.py:42
  307.4 38.3 %collective-permute-start.3 = (bf16[2,128,4,128]{1,3,2,0:T(8,128)(2,1)}, bf16[2,128,4,128]{1,3,2,0:T(8,128)(2,1)}, u32[]{:S(2)}, u32[]{:S(2)}) collective-permute-start(bf16[2,128,4,128]{1,3,2,0:T(8,128)(2,1)} %fusion.18), channel_id=1, source_target_pairs={{8,0},{16,8},{24,16},{32,24},{40,32},{48,40},{56,48},{64,56},{72,6... | collective-permute-start | bytes 786440 | tf_op jit(solution)/shard_map/ppermute | solution.py:42
  337.0 2.9 copy-start.2
  337.0 143.6 %all-reduce.24.cloned.1.call-start = ((), (), s32[]{:S(2)}) async-start(), calls=%async_computation.4 | async-start | bytes 1048576 | tf_op jit(solution)/shard_map/psum | solution.py:32
  339.9 2.5 copy-start.4
  341.2 1.4 copy-start.17
  341.2 2.4 copy-start.13
  397.2 1.3 copy-start.14
  397.2 41.0 %copy-start.5 = (bf16[256,4,128]{0,2,1:T(8,128)(2,1)S(1)}, bf16[256,4,128]{0,2,1:T(8,128)(2,1)}, u32[]{:S(2)}) copy-start(bf16[256,4,128]{0,2,1:T(8,128)(2,1)} %reshape.250) | copy-start | bytes 786436
  397.2 41.0 %copy-start.6 = (bf16[256,4,128]{0,2,1:T(8,128)(2,1)S(1)}, bf16[256,4,128]{0,2,1:T(8,128)(2,1)}, u32[]{:S(2)}) copy-start(bf16[256,4,128]{0,2,1:T(8,128)(2,1)} %reshape.248) | copy-start | bytes 786436
  (5 other events, 4.9 us)
Sparse Core Ops, SparseCore 0:
  67.8 34.5 all-reduce.17
  104.8 54.2 all-reduce.19
  161.5 81.1 all-reduce.21
  303.1 33.8 all-reduce.27
  339.5 57.6 all-reduce.25
  399.5 81.0 all-reduce.23
where the time goes:
time: 491 us; the launch traced here: 490 us
  waiting for transfers between devices  291 us (59%)
  blocking collectives  78.5 us (16%)
  local copies, waits for them, and re-layouts  64.2 us (13%)
  starting transfers between devices  18.6 us (4%)
  between operations  14.8 us (3%)
  matrix products  12.6 us (3%)
  other arithmetic  10.3 us (2%)
    psum x6, waiting for transfers between devices, hpsum(): value = lax.psum(value, name)  263 us
    psum x1, blocking collectives, hpsum(): value = lax.psum(value, name)  39.7 us
    all_gather x3, blocking collectives, hgather(): value = lax.all_gather(value, name, axis=0, tiled=True)  38.8 us
    all_to_all x1, waiting for transfers between devices, local(): lax.all_to_all(stacked, 'head', split_axis=2, concat_axis=1, tiled=True)  28.7 us
    unnamed x45, local copies, waits for them, and re-layouts  20.4 us
    scatter-add x1, local copies, waits for them, and re-layouts, local(): inner = inner.at[:, -1].add(from_right)  12 us
    ppermute x4, starting transfers between devices, shifted(): lax.ppermute(value, seq, [(s, s + steps) for s in range(leading, last)])  11.1 us
    all_to_all x2, local copies, waits for them, and re-layouts, local(): lax.all_to_all(stacked, 'head', split_axis=2, concat_axis=1, tiled=True)  10.2 us
  transfers between devices with their start and end apart: 11, of which 7 were waited for; matrix products, arithmetic and copies ran while one was open for 8% of the time, Pallas kernels for 0%

commit v1 on v0

--- a/solution.py
+++ b/solution.py
@@ -43,7 +43,12 @@
 
     def local(query_states, key_states, value_states, out_grad):
         stacked = jnp.stack([query_states, key_states, value_states, out_grad])
-        stacked = lax.all_to_all(stacked, "head", split_axis=2, concat_axis=1, tiled=True)
+        stacked = jnp.concatenate(
+            lax.all_to_all(
+                jnp.stack(jnp.split(stacked, lax.axis_size("head"), axis=2)), "head", 0, 0
+            ),
+            axis=1,
+        )
         local_rows = stacked.shape[1]
         head_count = stacked.shape[2] // HEAD_DIM
         block_count = local_rows // BLOCK

time: 491 us -> 474 us (0.965)
  local copies, waits for them, and re-layouts: 64.2 us -> 42.7 us
  waiting for transfers between devices: 291 us -> 298 us
    all_to_all x2 -> x1, local copies, waits for them, and re-layouts: 10.2 us -> 0.1 us  [local(): lax.all_to_all(jnp.stack(jnp.split(stacked, lax.axis_size('head'), axis=2...]
    unnamed x45 -> x44, local copies, waits for them, and re-layouts: 20.4 us -> 12.7 us
    psum x6, waiting for transfers between devices: 263 us -> 269 us  [hpsum(): value = lax.psum(value, name)]
  transfers between devices with their start and end apart: 11 -> 11, of which waited for: 7 -> 7; matrix products, arithmetic and copies ran while one was open for 8% -> 7% of each run, Pallas kernels for 0% -> 0%
where the time goes in v1:
time: 474 us; the launch traced here: 473 us
  waiting for transfers between devices  298 us (63%)
  blocking collectives  78.3 us (17%)
  local copies, waits for them, and re-layouts  42.7 us (9%)
  starting transfers between devices  18.6 us (4%)
  between operations  14.7 us (3%)
  matrix products  11.1 us (2%)
  other arithmetic  10.2 us (2%)
    psum x6, waiting for transfers between devices, hpsum(): value = lax.psum(value, name)  269 us
    psum x1, blocking collectives, hpsum(): value = lax.psum(value, name)  39.4 us
    all_gather x3, blocking collectives, hgather(): value = lax.all_gather(value, name, axis=0, tiled=True)  38.8 us
    all_to_all x1, waiting for transfers between devices, local(): lax.all_to_all(jnp.stack(jnp.split(stacked, lax.axis_size('head'), axis=2...  28.7 us
    unnamed x44, local copies, waits for them, and re-layouts  12.7 us
    scatter-add x1, local copies, waits for them, and re-layouts, local(): inner = inner.at[:, -1].add(from_right)  12 us
    ppermute x4, starting transfers between devices, shifted(): lax.ppermute(value, seq, [(s, s + steps) for s in range(leading, last)])  11.1 us
  transfers between devices with their start and end apart: 11, of which 7 were waited for; matrix products, arithmetic and copies ran while one was open for 7% of the time, Pallas kernels for 0%

profile of v1, /device:TPU:2, one launch (start us, length us, event | category | flops | bytes accessed | tf_op | source)
XLA Modules:
  0.0 473.3 jit_solution(3017845734140277190)
XLA Ops:
  13.8 7.1 %all-to-all-start = ((bf16[8,4,32,512]{3,2,1,0:T(8,128)(2,1)}), bf16[8,4,32,512]{3,2,1,0:T(8,128)(2,1)S(1)}, u32[]{:S(2)}, u32[]{:S(2)}) async-start(bf16[8,4,32,512]{3,2,1,0:T(8,128)(2,1)} %fusion.31), calls=%async_computation | async-start | bytes 2097152 | tf_op jit(solution)/shard_map/all_to_all | solution.py:47
  20.9 28.7 %all-to-all-done = bf16[8,4,32,512]{3,2,1,0:T(8,128)(2,1)S(1)} async-done(((bf16[8,4,32,512]{3,2,1,0:T(8,128)(2,1)}), bf16[8,4,32,512]{3,2,1,0:T(8,128)(2,1)S(1)}, u32[]{:S(2)}, u32[]{:S(2)}) %all-to-all-start) | async-done | bytes 1048608 | tf_op jit(solution)/shard_map/all_to_all | solution.py:47
  50.7 34.6 %all-reduce.18.cloned.1.call-done = bf16[4,128,512]{2,1,0:T(8,128)(2,1)} async-done(((bf16[4,128,512]{2,1,0:T(8,128)(2,1)}), bf16[4,128,512]{2,1,0:T(8,128)(2,1)}) %all-reduce.18.cloned.1.call-update) | async-done | bytes 524304 | tf_op jit(solution)/shard_map/psum | solution.py:32
  86.3 2.2 collective-permute-start
  88.5 3.4 collective-permute-start.1
  91.8 50.1 %all-reduce.20.cloned.1.call-done = bf16[4,128,512]{2,1,0:T(8,128)(2,1)} async-done(((bf16[4,128,512]{2,1,0:T(8,128)(2,1)}), bf16[4,128,512]{2,1,0:T(8,128)(2,1)}) %all-reduce.20.cloned.1.call-update) | async-done | bytes 524304 | tf_op jit(solution)/shard_map/psum | solution.py:32
  146.9 78.7 %all-reduce.22.cloned.1.call-done = bf16[4,128,512]{2,1,0:T(8,128)(2,1)} async-done(((bf16[4,128,512]{2,1,0:T(8,128)(2,1)}), bf16[4,128,512]{2,1,0:T(8,128)(2,1)}) %all-reduce.22.cloned.1.call-update) | async-done | bytes 524304 | tf_op jit(solution)/shard_map/psum | solution.py:32
  228.8 1.8 all-gather
  230.6 11.9 %all_gather.10 = f32[8,3,4,128]{3,2,1,0:T(4,128)S(1)} all-gather(f32[2,3,4,128]{3,2,1,0:T(4,128)S(1)} %bitcast.202), channel_id=1, replica_groups=mesh['sz'=8,'sx'=4,'sc'=2,'head'=8] {'sx'}, dimensions={0}, use_global_device_ids=true | all-gather | bytes 61440 | tf_op jit(solution)/shard_map/all_gather | solution.py:37
  242.5 25.1 %all_gather.11 = f32[64,3,4,128]{3,2,1,0:T(4,128)S(1)} all-gather(f32[8,3,4,128]{3,2,1,0:T(4,128)S(1)} %all_gather.10), channel_id=1, replica_groups=mesh['sz'=8,'sx'=4,'sc'=2,'head'=8] {'sz'}, dimensions={0}, use_global_device_ids=true | all-gather | bytes 442368 | tf_op jit(solution)/shard_map/all_gather | solution.py:37
  274.0 1.6 multiply_convert_fusion
  275.5 1.7 stack.99
  277.3 1.6 multiply_bitcast_fusion
  278.9 1.7 stack.98
  280.7 2.0 copy_dynamic-update-slice_fusion.1
  283.4 1.7 copy-done
  287.7 1.9 collective-permute-start.2
  290.4 3.6 collective-permute-start.3
  294.0 25.9 %all-reduce.28.cloned.1.call-done = (f32[128,4,128]{0,2,1:T(8,128)}, f32[128,4,128]{0,2,1:T(8,128)}, f32[128,4,128]{0,2,1:T(8,128)}, f32[128,4,128]{0,2,1:T(8,128)}) async-done(((f32[128,4,128]{0,2,1:T(8,128)}, f32[128,4,128]{0,2,1:T(8,128)}, f32[128,4,128]{0,2,1:T(8,128)}, f32[128,4,128]{0,2,1:T(8,128)}), (f32[128,4,128]{0,2,1:T(8,128)}, f32[128,4,128]{0,2,1:T(8,128)}, f32[128,4,128]{0,2,1:T(8,128)}, ...) | async-done | bytes 1048592 | tf_op jit(solution)/shard_map/psum | solution.py:32
  320.2 1.9 fusion.1
  328.7 12.0 %scatter-add.9 = f32[2,2,128,4,128]{2,1,4,3,0:T(2,128)S(1)} dynamic-update-slice(f32[2,2,128,4,128]{2,1,4,3,0:T(2,128)S(1)} %copy.100, f32[2,1,128,4,128]{2,1,4,3,0:T(1,128)S(1)} %add.147, s32[]{:T(128)} %constant.93.clone.1, s32[]{:T(128)} %constant.98.clone.1, s32[]{:T(128)} %constant.93.clone.1, s32[]{:T(128)} %constant.93.clone.1, s32[]{:T(128)} %constant.93.clone.1) | dynamic-update-slice | bytes 1048580 | tf_op jit(solution)/shard_map/scatter-add | solution.py:204
  341.6 38.6 %all-reduce.26.cloned.1.call-done = (f32[128,4,128]{0,2,1:T(8,128)}, f32[128,4,128]{0,2,1:T(8,128)}, f32[128,4,128]{0,2,1:T(8,128)}, f32[128,4,128]{0,2,1:T(8,128)}) async-done(((f32[128,4,128]{0,2,1:T(8,128)}, f32[128,4,128]{0,2,1:T(8,128)}, f32[128,4,128]{0,2,1:T(8,128)}, f32[128,4,128]{0,2,1:T(8,128)}), (f32[128,4,128]{0,2,1:T(8,128)}, f32[128,4,128]{0,2,1:T(8,128)}, f32[128,4,128]{0,2,1:T(8,128)}, ...) | async-done | bytes 1048592 | tf_op jit(solution)/shard_map/psum | solution.py:32
  380.4 39.4 %all-reduce.29 = (bf16[128,4,128]{0,2,1:T(8,128)(2,1)S(1)}, bf16[128,4,128]{0,2,1:T(8,128)(2,1)S(1)}) all-reduce(f32[128,4,128]{0,2,1:T(8,128)} %get-tuple-element.46, f32[128,4,128]{0,2,1:T(8,128)} %get-tuple-element.47), channel_id=1, replica_groups=mesh['sz'=8,'sx'=4,'sc'=2,'head'=8] {'sz'}, use_global_device_ids=true, to_apply=%region_10.11 | all-reduce | flops 131072 | bytes 786432 | tf_op jit(solution)/shard_map/psum | solution.py:32
  422.6 41.0 %all-reduce.24.cloned.1.call-done = (f32[128,4,128]{0,2,1:T(8,128)}, f32[128,4,128]{0,2,1:T(8,128)}) async-done(((f32[128,4,128]{0,2,1:T(8,128)}, f32[128,4,128]{0,2,1:T(8,128)}), (f32[128,4,128]{0,2,1:T(8,128)}, f32[128,4,128]{0,2,1:T(8,128)})) %all-reduce.24.cloned.1.call-update) | async-done | bytes 524304 | tf_op jit(solution)/shard_map/psum | solution.py:32
  (137 shorter events, 40.1 us)
Async XLA Ops:
  13.8 35.8 %all-to-all-start = ((bf16[8,4,32,512]{3,2,1,0:T(8,128)(2,1)}), bf16[8,4,32,512]{3,2,1,0:T(8,128)(2,1)S(1)}, u32[]{:S(2)}, u32[]{:S(2)}) async-start(bf16[8,4,32,512]{3,2,1,0:T(8,128)(2,1)} %fusion.31), calls=%async_computation | async-start | bytes 2097152 | tf_op jit(solution)/shard_map/all_to_all | solution.py:47
  20.9 64.4 %all-reduce.18.cloned.1.call-start = ((), (), s32[]{:S(2)}) async-start(), calls=%async_computation.1 | async-start | bytes 1048576 | tf_op jit(solution)/shard_map/psum | solution.py:32
  50.6 91.4 %all-reduce.20.cloned.1.call-start = ((), (), s32[]{:S(2)}) async-start(), calls=%async_computation.2 | async-start | bytes 1048576 | tf_op jit(solution)/shard_map/psum | solution.py:32
  85.3 140.3 %all-reduce.22.cloned.1.call-start = ((), (), s32[]{:S(2)}) async-start(), calls=%async_computation.3 | async-start | bytes 1048576 | tf_op jit(solution)/shard_map/psum | solution.py:32
  86.3 57.6 %collective-permute-start = (bf16[2,128,512]{2,1,0:T(8,128)(2,1)}, bf16[2,128,512]{2,1,0:T(8,128)(2,1)}, u32[]{:S(2)}, u32[]{:S(2)}) collective-permute-start(bf16[2,128,512]{2,1,0:T(8,128)(2,1)} %get-tuple-element.77), channel_id=1, source_target_pairs={{0,8},{8,16},{16,24},{24,32},{32,40},{40,48},{48,56},{56,64},{64,7... | collective-permute-start | bytes 786440 | tf_op jit(solution)/shard_map/ppermute | solution.py:42
  88.5 55.4 %collective-permute-start.1 = (bf16[2,128,512]{2,1,0:T(8,128)(2,1)S(1)}, bf16[2,128,512]{2,1,0:T(8,128)(2,1)}, u32[]{:S(2)}, u32[]{:S(2)}) collective-permute-start(bf16[2,128,512]{2,1,0:T(8,128)(2,1)S(1)} %get-tuple-element.78), channel_id=1, source_target_pairs={{8,0},{16,8},{24,16},{32,24},{40,32},{48,40},{56,48},{64,56},{72,6... | collective-permute-start | bytes 786440 | tf_op jit(solution)/shard_map/ppermute | solution.py:42
  142.0 178.0 %all-reduce.28.cloned.1.call-start = ((), (), s32[]{:S(2)}) async-start(), calls=%async_computation.6 | async-start | bytes 2097152 | tf_op jit(solution)/shard_map/psum | solution.py:32
  143.6 126.5 %copy-start.8 = (bf16[2,128,4,128]{3,1,2,0:T(8,128)(2,1)}, bf16[2,128,4,128]{3,1,2,0:T(8,128)(2,1)S(1)}, u32[]{:S(2)}) copy-start(bf16[2,128,4,128]{3,1,2,0:T(8,128)(2,1)S(1)} %copy.85) | copy-start | bytes 786436
  145.1 125.0 %copy-start.9 = (bf16[2,128,4,128]{3,1,2,0:T(8,128)(2,1)}, bf16[2,128,4,128]{3,1,2,0:T(8,128)(2,1)S(1)}, u32[]{:S(2)}) copy-start(bf16[2,128,4,128]{3,1,2,0:T(8,128)(2,1)S(1)} %copy.84) | copy-start | bytes 786436
  146.9 123.3 %copy-start.10 = (bf16[2,128,4,128]{3,1,2,0:T(8,128)(2,1)}, bf16[2,128,4,128]{3,1,2,0:T(8,128)(2,1)S(1)}, u32[]{:S(2)}) copy-start(bf16[2,128,4,128]{3,1,2,0:T(8,128)(2,1)S(1)} %copy.86) | copy-start | bytes 786436
  227.8 41.1 %copy-start.3 = (bf16[1,128,512]{1,2,0:T(8,128)(2,1)}, bf16[1,128,512]{1,2,0:T(8,128)(2,1)S(1)}, u32[]{:S(2)}) copy-start(bf16[1,128,512]{1,2,0:T(8,128)(2,1)S(1)} %copy.71) | copy-start | bytes 393220
  271.5 1.0 copy-start.11
  271.5 1.1 copy-start.13
  271.6 1.2 copy-start.14
  280.7 2.2 copy-start.1
  283.2 2.0 copy-start
  286.0 94.3 %all-reduce.26.cloned.1.call-start = ((), (), s32[]{:S(2)}) async-start(), calls=%async_computation.5 | async-start | bytes 2097152 | tf_op jit(solution)/shard_map/psum | solution.py:32
  287.7 38.5 %collective-permute-start.2 = (bf16[2,128,4,128]{1,3,2,0:T(8,128)(2,1)}, bf16[2,128,4,128]{1,3,2,0:T(8,128)(2,1)S(1)}, u32[]{:S(2)}, u32[]{:S(2)}) collective-permute-start(bf16[2,128,4,128]{1,3,2,0:T(8,128)(2,1)} %fusion.17), channel_id=1, source_target_pairs={{0,8},{8,16},{16,24},{24,32},{32,40},{40,48},{48,56},{56,64},{64,7... | collective-permute-start | bytes 786440 | tf_op jit(solution)/shard_map/ppermute | solution.py:42
  290.4 36.8 %collective-permute-start.3 = (bf16[2,128,4,128]{1,3,2,0:T(8,128)(2,1)}, bf16[2,128,4,128]{1,3,2,0:T(8,128)(2,1)}, u32[]{:S(2)}, u32[]{:S(2)}) collective-permute-start(bf16[2,128,4,128]{1,3,2,0:T(8,128)(2,1)} %fusion.18), channel_id=1, source_target_pairs={{8,0},{16,8},{24,16},{32,24},{40,32},{48,40},{56,48},{64,56},{72,6... | collective-permute-start | bytes 786440 | tf_op jit(solution)/shard_map/ppermute | solution.py:42
  320.0 2.2 copy-start.2
  320.0 143.7 %all-reduce.24.cloned.1.call-start = ((), (), s32[]{:S(2)}) async-start(), calls=%async_computation.4 | async-start | bytes 1048576 | tf_op jit(solution)/shard_map/psum | solution.py:32
  322.1 1.7 copy-start.4
  323.5 1.6 copy-start.12
  380.2 39.6 %copy-start.5 = (bf16[256,4,128]{0,2,1:T(8,128)(2,1)S(1)}, bf16[256,4,128]{0,2,1:T(8,128)(2,1)}, u32[]{:S(2)}) copy-start(bf16[256,4,128]{0,2,1:T(8,128)(2,1)} %reshape.258) | copy-start | bytes 786436
  (2 other events, 1.6 us)
Sparse Core Ops, SparseCore 0:
  50.7 34.5 all-reduce.17
  87.7 54.2 all-reduce.19
  144.4 81.1 all-reduce.21
  286.1 33.8 all-reduce.27
  322.5 57.7 all-reduce.25
  382.5 81.1 all-reduce.23
